TPU v7x, 512 devices: a whole 4x4x16 slice. The times are simulated.
512 devices in a mesh: ctx: 32 (over x, z_lo, core), tp: 16 (over y, z_hi).
Axes of the slice: x: 4, y: 4, z: 16 (z_hi: 4, z_lo: 4; z = z_hi * 4 + z_lo), core: 2. Of those that a mesh axis runs over, the one named last changes fastest.
Arguments:
- attention_out: bfloat16 [512, 8192], P('ctx', 'tp'), may hold values from -6 to 6
- w_out: bfloat16 [8192, 8192], P('tp', 'ctx'), may hold values from -0.0625 to 0.0625
- residual: bfloat16 [512, 8192], P(('ctx', 'tp')), may hold values from -6 to 6
- norm_gain: float32 [8192], replicated, may hold values from 0.1 to 1.9
- w_gate: bfloat16 [28672, 8192], P(('ctx', 'tp')), may hold values from -0.0625 to 0.0625
- w_up: bfloat16 [28672, 8192], P(('ctx', 'tp')), may hold values from -0.0625 to 0.0625
- w_down: bfloat16 [32, 896, 8192], P(None, 'tp', 'ctx'), may hold values from -0.03125 to 0.03125
Outputs:
- mixed: bfloat16 [512, 8192], P(('ctx', 'tp'))
All inputs are finite; a program needn't handle non-finite values.
Results may differ from a plain program's by a relative error of at most 0.02.
Values may be sent and summed in bfloat16 or wider, within the bound.
No kernel may reach another device: no remote copies, remote signals or barrier semaphores. Data moves between devices by JAX's collectives and lax.ppermute only.
A program may use at most 64 MiB of HBM per device.

v0:
```python
import jax
import jax.numpy as jnp
from jax import lax
from jax.sharding import PartitionSpec as P


def owner_order(partial_value, ctx_count, tp_count, row_count):
    col_count = partial_value.shape[1]
    grouped = partial_value.reshape(ctx_count, tp_count, row_count, col_count)
    return jnp.transpose(grouped, (1, 0, 2, 3)).reshape(tp_count * ctx_count * row_count, col_count)


def shards(attention_out, w_out, residual, norm_gain, w_gate, w_up, w_down):
    row_count = residual.shape[0]
    ctx_count = lax.axis_size("ctx")
    tp_count = lax.axis_size("tp")
    unit_count = w_gate.shape[0]
    col_count = w_down.shape[2]
    partial_value = jnp.dot(
        lax.all_gather(attention_out, "ctx", axis=0, tiled=True),
        w_out,
        preferred_element_type=jnp.float32,
    )
    summed = lax.psum_scatter(
        owner_order(partial_value, ctx_count, tp_count, row_count).astype(jnp.bfloat16),
        "tp",
        scatter_dimension=0,
        tiled=True,
    ).astype(jnp.float32)
    proj = lax.all_to_all(
        summed.astype(jnp.bfloat16), "ctx", split_axis=0, concat_axis=1, tiled=True
    ).astype(summed.dtype)
    carried = residual.astype(jnp.float32) + proj
    mean_square = jnp.mean(carried * carried, axis=-1, keepdims=True)
    normed = (carried * lax.rsqrt(mean_square + 1e-05) * norm_gain).astype(jnp.bfloat16)
    paired = jnp.concatenate([w_gate, w_up], axis=0)
    group = lax.all_gather(normed, "tp", axis=0, tiled=True)
    gate_up = lax.dot_general(
        lax.all_gather(group, "ctx", axis=0, tiled=True),
        paired,
        (((1,), (1,)), ((), ())),
        preferred_element_type=jnp.float32,
    )
    gate_part = gate_up[:, :unit_count]
    up_part = gate_up[:, unit_count:]
    hidden = (jax.nn.silu(gate_part) * up_part).astype(jnp.bfloat16)
    flat_down = w_down.reshape(ctx_count * unit_count, col_count)
    partial_down = jnp.dot(
        lax.all_gather(hidden, "ctx", axis=1, tiled=True),
        flat_down,
        preferred_element_type=jnp.float32,
    )
    reduced = lax.psum_scatter(
        owner_order(partial_down, ctx_count, tp_count, row_count).astype(jnp.bfloat16),
        "tp",
        scatter_dimension=0,
        tiled=True,
    ).astype(jnp.float32)
    down = lax.all_to_all(
        reduced.astype(jnp.bfloat16), "ctx", split_axis=0, concat_axis=1, tiled=True
    ).astype(reduced.dtype)
    return (carried + down).astype(jnp.bfloat16)


def solution(mesh):
    in_specs = (
        P("ctx", "tp"),
        P("tp", "ctx"),
        P(("ctx", "tp"), None),
        P(),
        P(("ctx", "tp"), None),
        P(("ctx", "tp"), None),
        P(None, "tp", "ctx"),
    )
    out_specs = P(("ctx", "tp"), None)
    return jax.shard_map(shards, mesh=mesh, in_specs=in_specs, out_specs=out_specs, check_vma=False)
```

profile of v0, /device:TPU:1, one launch (start us, length us, event | category | flops | bytes accessed | tf_op | source)
XLA Modules:
  0.0 513.3 jit_solution(6987445112993718375)
XLA Ops:
  6.5 0.0 copy-start
  6.5 0.0 reduce-scatter.3.cloned.1.call-start
  6.5 48.2 %all_gather.12 = bf16[512,512]{1,0:T(8,128)(2,1)S(1)} all-gather(bf16[16,512]{1,0:T(8,128)(2,1)} %param.7), channel_id=1, replica_groups=mesh['ctx'=32,'tp'=16] {'ctx'}, dimensions={0}, use_global_device_ids=true | all-gather | bytes 540672 | tf_op jit(solution)/shard_map/all_gather | solution.py:20
  54.7 1.4 convolution_convert_fusion.1
  56.1 0.8 copy.12
  56.9 0.0 reduce-scatter.3.cloned.1.call-update
  56.9 0.0 all-gather.4.cloned.1.call-start
  56.9 108.8 %reduce-scatter.3.cloned.1.call-done = bf16[32,256]{1,0:T(8,128)(2,1)} async-done(((bf16[512,256]{1,0:T(8,128)(2,1)}), bf16[32,256]{1,0:T(8,128)(2,1)}) %reduce-scatter.3.cloned.1.call-update) | async-done | bytes 16400 | tf_op jit(solution)/shard_map/reduce_scatter | solution.py:24
  165.8 0.5 broadcast.4
  166.3 1.4 reduce.1
  167.6 14.4 %all_to_all.26 = bf16[32,2,128]{2,1,0:T(2,128)(2,1)S(1)} all-to-all(bf16[32,2,128]{2,1,0:T(2,128)(2,1)S(1)} %reshape.72), channel_id=1, replica_groups=mesh['ctx'=32,'tp'=16] {'ctx'}, dimensions={0} | all-to-all | bytes 32768 | tf_op jit(solution)/shard_map/all_to_all | solution.py:30
  182.1 0.7 multiply_reduce_fusion
  183.5 0.1 convert_bitcast_fusion
  183.6 50.3 %all-gather = bf16[16,1,8192]{2,1,0:T(2,128)(2,1)S(1)} all-gather(bf16[1,1,8192]{2,1,0:T(2,128)(2,1)S(1)} %convert_bitcast_fusion), channel_id=1, replica_groups=mesh['ctx'=32,'tp'=16] {'tp'}, dimensions={0}, use_global_device_ids=true | all-gather | bytes 278528 | tf_op jit(solution)/shard_map/all_gather | solution.py:37
  233.9 1.0 copy.19
  234.9 0.0 all-gather.4.cloned.1.call-update
  234.9 0.0 all-gather.6.cloned.1.call-start
  235.0 71.6 %all-gather.4.cloned.1.call-done = bf16[512,8192]{1,0:T(8,128)(2,1)} async-done(((bf16[16,8192]{1,0:T(8,128)(2,1)}), bf16[512,8192]{1,0:T(8,128)(2,1)}) %all-gather.4.cloned.1.call-update) | async-done | bytes 8388624 | tf_op jit(solution)/shard_map/all_gather | solution.py:39
  306.5 6.2 %fusion = f32[512,112]{0,1:T(8,128)S(1)} fusion(bf16[512,8192]{1,0:T(8,128)(2,1)} %all-gather.4.cloned.1.call-done, bf16[56,8192]{1,0:T(8,128)(2,1)S(1)} %copy-done.3, bf16[56,8192]{1,0:T(8,128)(2,1)S(1)} %copy-done.4), kind=kOutput, calls=%fused_computation | convolution fusion | flops 943194112 | bytes 10452992 | tf_op jit(solution)/shard_map/dot_general | solution.py:38
  312.8 0.7 fusion.5
  313.4 0.0 all-gather.6.cloned.1.call-update
  313.5 0.0 reduce-scatter.5.cloned.1.call-start
  313.5 64.0 %all-gather.6.cloned.1.call-done = bf16[512,1792]{0,1:T(8,128)(2,1)} async-done(((bf16[512,56]{0,1:T(8,128)(2,1)}), bf16[512,1792]{0,1:T(8,128)(2,1)}) %all-gather.6.cloned.1.call-update) | async-done | bytes 1835024 | tf_op jit(solution)/shard_map/all_gather | solution.py:49
  377.5 2.8 copy.14
  380.3 0.0 copy-done
  380.3 0.6 fusion.4
  380.9 0.8 copy.15
  381.7 0.0 reduce-scatter.5.cloned.1.call-update
  381.7 108.5 %reduce-scatter.5.cloned.1.call-done = bf16[32,256]{1,0:T(8,128)(2,1)} async-done(((bf16[512,256]{1,0:T(8,128)(2,1)}), bf16[32,256]{1,0:T(8,128)(2,1)}) %reduce-scatter.5.cloned.1.call-update) | async-done | bytes 16400 | tf_op jit(solution)/shard_map/reduce_scatter | solution.py:53
  490.3 1.4 reduce.2
  491.6 14.4 %all_to_all.27 = bf16[32,2,128]{2,1,0:T(2,128)(2,1)S(1)} all-to-all(bf16[32,2,128]{2,1,0:T(2,128)(2,1)S(1)} %reshape.74), channel_id=1, replica_groups=mesh['ctx'=32,'tp'=16] {'ctx'}, dimensions={0} | all-to-all | bytes 32768 | tf_op jit(solution)/shard_map/all_to_all | solution.py:59
  506.1 0.7 fusion.6
  (12 shorter events, 0.1 us)
Async XLA Ops:
  6.5 373.7 %copy-start = (bf16[32,56,256]{2,1,0:T(8,128)(2,1)S(1)}, bf16[32,56,256]{2,1,0:T(8,128)(2,1)}, u32[]{:S(2)}) copy-start(bf16[32,56,256]{2,1,0:T(8,128)(2,1)} %param.13) | copy-start | bytes 2752516
  6.5 175.5 %copy-start.1 = (bf16[1,8192]{1,0:T(2,128)(2,1)S(1)}, bf16[1,8192]{1,0:T(2,128)(2,1)}, u32[]{:S(2)}) copy-start(bf16[1,8192]{1,0:T(2,128)(2,1)} %param.9) | copy-start | bytes 49156
  6.5 176.9 %copy-start.2 = (f32[8192]{0:T(1024)S(1)}, f32[8192]{0:T(1024)}, u32[]{:S(2)}) copy-start(f32[8192]{0:T(1024)} %param.10) | copy-start | bytes 98308
  6.5 159.2 %reduce-scatter.3.cloned.1.call-start = ((), (), s32[]{:S(2)}) async-start(), calls=%async_computation.4 | async-start | bytes 278528 | tf_op jit(solution)/shard_map/reduce_scatter | solution.py:24
  54.7 251.8 %copy-start.3 = (bf16[56,8192]{1,0:T(8,128)(2,1)S(1)}, bf16[56,8192]{1,0:T(8,128)(2,1)}, u32[]{:S(2)}) copy-start(bf16[56,8192]{1,0:T(8,128)(2,1)} %param.12) | copy-start | bytes 2752516
  54.7 251.8 %copy-start.4 = (bf16[56,8192]{1,0:T(8,128)(2,1)S(1)}, bf16[56,8192]{1,0:T(8,128)(2,1)}, u32[]{:S(2)}) copy-start(bf16[56,8192]{1,0:T(8,128)(2,1)} %param.11) | copy-start | bytes 2752516
  56.9 249.6 %all-gather.4.cloned.1.call-start = ((), (), s32[]{:S(2)}) async-start(), calls=%async_computation.5 | async-start | bytes 8650752 | tf_op jit(solution)/shard_map/all_gather | solution.py:39
  234.9 142.6 %all-gather.6.cloned.1.call-start = ((), (), s32[]{:S(2)}) async-start(), calls=%async_computation.6 | async-start | bytes 1892352 | tf_op jit(solution)/shard_map/all_gather | solution.py:49
  313.5 176.8 %reduce-scatter.5.cloned.1.call-start = ((), (), s32[]{:S(2)}) async-start(), calls=%async_computation.7 | async-start | bytes 278528 | tf_op jit(solution)/shard_map/reduce_scatter | solution.py:53
Sparse Core Ops, SparseCore 0:
  57.0 108.6 reduce-scatter.2
  235.0 71.4 all-gather.3
  313.6 63.8 all-gather.5
  381.9 108.2 reduce-scatter.4
where the time goes:
time: 514 us; the launch traced here: 513 us
  waiting for transfers between devices  353 us (69%)
  blocking collectives  127 us (25%)
  between operations  13.9 us (3%)
  matrix products  8.23 us (2%)
  local copies, waits for them, and re-layouts  5.9 us (1%)
    reduce_scatter x1, waiting for transfers between devices, shards(): lax.psum_scatter(owner_order(partial_value, ctx_count, tp_count, row_coun...  109 us
    reduce_scatter x1, waiting for transfers between devices, shards(): lax.psum_scatter(owner_order(partial_down, ctx_count, tp_count, row_count...  109 us
    all_gather x1, waiting for transfers between devices, shards(): lax.all_gather(group, 'ctx', axis=0, tiled=True)  71.6 us
    all_gather x1, waiting for transfers between devices, shards(): lax.all_gather(hidden, 'ctx', axis=1, tiled=True)  64 us
    all_gather x1, blocking collectives, shards(): group = lax.all_gather(normed, 'tp', axis=0, tiled=True)  50.3 us
    all_gather x1, blocking collectives, shards(): lax.all_gather(attention_out, 'ctx', axis=0, tiled=True)  48.2 us
    all_to_all x1, blocking collectives, shards(): lax.all_to_all(reduced.astype(jnp.bfloat16), 'ctx', split_axis=0, concat_...  14.4 us
    all_to_all x1, blocking collectives, shards(): lax.all_to_all(summed.astype(jnp.bfloat16), 'ctx', split_axis=0, concat_a...  14.4 us
  transfers between devices with their start and end apart: 4, of which 4 were waited for; matrix products, arithmetic and copies ran while one was open for 0% of the time, Pallas kernels for 0%

commit v1 on v0

--- a/solution.py
+++ b/solution.py
@@ -46,7 +46,9 @@
     hidden = (jax.nn.silu(gate_part) * up_part).astype(jnp.bfloat16)
     flat_down = w_down.reshape(ctx_count * unit_count, col_count)
     partial_down = jnp.dot(
-        lax.all_gather(hidden, "ctx", axis=1, tiled=True),
+        jnp.concatenate(
+            lax.all_to_all(jnp.stack([hidden] * lax.axis_size("ctx")), "ctx", 0, 0), axis=1
+        ),
         flat_down,
         preferred_element_type=jnp.float32,
     )

time: 514 us -> 509 us (level)
  waiting for transfers between devices: 353 us -> 288 us
  blocking collectives: 127 us -> 178 us
  local copies, waits for them, and re-layouts: 5.9 us -> 16.9 us
    all_gather x1 -> x0, waiting for transfers between devices: 64 us -> none  [shards(): lax.all_gather(hidden, 'ctx', axis=1, tiled=True)]
    all_to_all x0 -> x1, blocking collectives: none -> 50.4 us  [shards(): lax.all_to_all(jnp.stack([hidden] * lax.axis_size('ctx')), 'ctx', 0, 0)]
    dot_general x0 -> x1, local copies, waits for them, and re-layouts: none -> 7.03 us  [shards(): jnp.dot(jnp.concatenate(lax.all_to_all(jnp.stack([hidden] * lax.axis_size...]
    reshape x0 -> x1, local copies, waits for them, and re-layouts: none -> 6.63 us  [shards(): jnp.concatenate(lax.all_to_all(jnp.stack([hidden] * lax.axis_size('ctx'))...]
  transfers between devices with their start and end apart: 4 -> 3, of which waited for: 4 -> 3; matrix products, arithmetic and copies ran while one was open for 0% -> 0% of each run, Pallas kernels for 0% -> 0%
where the time goes in v1:
time: 509 us
  waiting for transfers between devices  288 us (57%)
  blocking collectives  178 us (35%)
  local copies, waits for them, and re-layouts  16.9 us (3%)
  between operations  13.9 us (3%)
  matrix products  8.23 us (2%)
    reduce_scatter x1, waiting for transfers between devices, shards(): lax.psum_scatter(owner_order(partial_value, ctx_count, tp_count, row_coun...  109 us
    reduce_scatter x1, waiting for transfers between devices, shards(): lax.psum_scatter(owner_order(partial_down, ctx_count, tp_count, row_count...  107 us
    all_gather x1, waiting for transfers between devices, shards(): lax.all_gather(group, 'ctx', axis=0, tiled=True)  71.6 us
    all_to_all x1, blocking collectives, shards(): lax.all_to_all(jnp.stack([hidden] * lax.axis_size('ctx')), 'ctx', 0, 0)  50.4 us
    all_gather x1, blocking collectives, shards(): group = lax.all_gather(normed, 'tp', axis=0, tiled=True)  50.3 us
    all_gather x1, blocking collectives, shards(): lax.all_gather(attention_out, 'ctx', axis=0, tiled=True)  48.2 us
    all_to_all x1, blocking collectives, shards(): lax.all_to_all(reduced.astype(jnp.bfloat16), 'ctx', split_axis=0, concat_...  14.4 us
    all_to_all x1, blocking collectives, shards(): lax.all_to_all(summed.astype(jnp.bfloat16), 'ctx', split_axis=0, concat_a...  14.4 us
  transfers between devices with their start and end apart: 3, of which 3 were waited for; matrix products, arithmetic and copies ran while one was open for 0% of the time, Pallas kernels for 0%

profile of v1, /device:TPU:1, one launch (start us, length us, event | category | flops | bytes accessed | tf_op | source)
XLA Modules:
  0.0 508.8 jit_solution(4308372482130777843)
XLA Ops:
  6.5 0.0 copy-start
  6.5 0.0 reduce-scatter.3.cloned.1.call-start
  6.5 48.2 %all_gather.9 = bf16[512,512]{1,0:T(8,128)(2,1)S(1)} all-gather(bf16[16,512]{1,0:T(8,128)(2,1)} %param.7), channel_id=1, replica_groups=mesh['ctx'=32,'tp'=16] {'ctx'}, dimensions={0}, use_global_device_ids=true | all-gather | bytes 540672 | tf_op jit(solution)/shard_map/all_gather | solution.py:20
  54.7 1.4 convolution_convert_fusion.1
  56.1 0.8 copy.12
  56.9 0.0 reduce-scatter.3.cloned.1.call-update
  56.9 0.0 all-gather.3.cloned.1.call-start
  57.0 108.8 %reduce-scatter.3.cloned.1.call-done = bf16[32,256]{1,0:T(8,128)(2,1)} async-done(((bf16[512,256]{1,0:T(8,128)(2,1)}), bf16[32,256]{1,0:T(8,128)(2,1)}) %reduce-scatter.3.cloned.1.call-update) | async-done | bytes 16400 | tf_op jit(solution)/shard_map/reduce_scatter | solution.py:24
  165.8 0.5 broadcast.6
  166.3 1.4 reduce.1
  167.7 14.4 %all_to_all.31 = bf16[32,2,128]{2,1,0:T(2,128)(2,1)S(1)} all-to-all(bf16[32,2,128]{2,1,0:T(2,128)(2,1)S(1)} %reshape.80), channel_id=1, replica_groups=mesh['ctx'=32,'tp'=16] {'ctx'}, dimensions={0} | all-to-all | bytes 32768 | tf_op jit(solution)/shard_map/all_to_all | solution.py:30
  182.0 0.0 copy-done.1
  182.1 0.7 multiply_reduce_fusion
  183.6 0.1 convert_bitcast_fusion
  183.6 50.3 %all-gather = bf16[16,1,8192]{2,1,0:T(2,128)(2,1)S(1)} all-gather(bf16[1,1,8192]{2,1,0:T(2,128)(2,1)S(1)} %convert_bitcast_fusion), channel_id=1, replica_groups=mesh['ctx'=32,'tp'=16] {'tp'}, dimensions={0}, use_global_device_ids=true | all-gather | bytes 278528 | tf_op jit(solution)/shard_map/all_gather | solution.py:37
  234.0 1.0 copy.19
  235.0 0.0 all-gather.3.cloned.1.call-update
  235.0 0.0 reduce-scatter.5.cloned.1.call-start
  235.0 71.6 %all-gather.3.cloned.1.call-done = bf16[512,8192]{1,0:T(8,128)(2,1)} async-done(((bf16[16,8192]{1,0:T(8,128)(2,1)}), bf16[512,8192]{1,0:T(8,128)(2,1)}) %all-gather.3.cloned.1.call-update) | async-done | bytes 8388624 | tf_op jit(solution)/shard_map/all_gather | solution.py:39
  306.6 0.0 copy-done.4
  306.6 6.2 %fusion = f32[512,112]{0,1:T(8,128)S(1)} fusion(bf16[512,8192]{1,0:T(8,128)(2,1)} %all-gather.3.cloned.1.call-done, bf16[56,8192]{1,0:T(8,128)(2,1)S(1)} %copy-done.3, bf16[56,8192]{1,0:T(8,128)(2,1)S(1)} %copy-done.4), kind=kOutput, calls=%fused_computation | convolution fusion | flops 943194112 | bytes 10452992 | tf_op jit(solution)/shard_map/dot_general | solution.py:38
  312.9 0.1 stack.2
  313.0 50.4 %all_to_all.32 = bf16[32,512,56]{1,2,0:T(8,128)(2,1)S(1)} all-to-all(bf16[32,512,56]{1,2,0:T(8,128)(2,1)S(1)} %stack.2), channel_id=1, replica_groups=mesh['ctx'=32,'tp'=16] {'ctx'}, dimensions={0} | all-to-all | bytes 3670016 | tf_op jit(solution)/shard_map/all_to_all | solution.py:50
  363.4 6.6 %copy.14 = bf16[512,32,56]{2,1,0:T(8,128)(2,1)} copy(bf16[512,32,56]{0,2,1:T(8,128)(2,1)S(1)} %bitcast.31) | data formatting | bytes 3670016 | tf_op jit(solution)/shard_map/reshape | solution.py:49
  370.0 7.0 %dot_general.13 = bf16[32,16,1792]{2,1,0:T(8,128)(2,1)S(1)} reshape(bf16[512,32,56]{2,1,0:T(8,128)(2,1)} %copy.14) | data formatting | bytes 3670016 | tf_op jit(solution)/shard_map/dot_general | solution.py:48
  377.1 0.6 fusion.4
  377.7 0.8 copy.15
  378.5 0.0 reduce-scatter.5.cloned.1.call-update
  378.5 107.3 %reduce-scatter.5.cloned.1.call-done = bf16[32,256]{1,0:T(8,128)(2,1)} async-done(((bf16[512,256]{1,0:T(8,128)(2,1)}), bf16[32,256]{1,0:T(8,128)(2,1)}) %reduce-scatter.5.cloned.1.call-update) | async-done | bytes 16400 | tf_op jit(solution)/shard_map/reduce_scatter | solution.py:55
  485.8 1.4 reduce.2
  487.2 14.4 %all_to_all.33 = bf16[32,2,128]{2,1,0:T(2,128)(2,1)S(1)} all-to-all(bf16[32,2,128]{2,1,0:T(2,128)(2,1)S(1)} %reshape.82), channel_id=1, replica_groups=mesh['ctx'=32,'tp'=16] {'ctx'}, dimensions={0} | all-to-all | bytes 32768 | tf_op jit(solution)/shard_map/all_to_all | solution.py:61
  501.6 0.7 fusion.6
  (12 shorter events, 0.1 us)
Async XLA Ops:
  6.5 370.5 %copy-start = (bf16[32,56,256]{2,1,0:T(8,128)(2,1)S(1)}, bf16[32,56,256]{2,1,0:T(8,128)(2,1)}, u32[]{:S(2)}) copy-start(bf16[32,56,256]{2,1,0:T(8,128)(2,1)} %param.13) | copy-start | bytes 2752516
  6.5 175.5 %copy-start.1 = (bf16[1,8192]{1,0:T(2,128)(2,1)S(1)}, bf16[1,8192]{1,0:T(2,128)(2,1)}, u32[]{:S(2)}) copy-start(bf16[1,8192]{1,0:T(2,128)(2,1)} %param.9) | copy-start | bytes 49156
  6.5 177.0 %copy-start.2 = (f32[8192]{0:T(1024)S(1)}, f32[8192]{0:T(1024)}, u32[]{:S(2)}) copy-start(f32[8192]{0:T(1024)} %param.10) | copy-start | bytes 98308
  6.5 159.2 %reduce-scatter.3.cloned.1.call-start = ((), (), s32[]{:S(2)}) async-start(), calls=%async_computation.5 | async-start | bytes 278528 | tf_op jit(solution)/shard_map/reduce_scatter | solution.py:24
  54.7 251.9 %copy-start.3 = (bf16[56,8192]{1,0:T(8,128)(2,1)S(1)}, bf16[56,8192]{1,0:T(8,128)(2,1)}, u32[]{:S(2)}) copy-start(bf16[56,8192]{1,0:T(8,128)(2,1)} %param.12) | copy-start | bytes 2752516
  54.7 251.9 %copy-start.4 = (bf16[56,8192]{1,0:T(8,128)(2,1)S(1)}, bf16[56,8192]{1,0:T(8,128)(2,1)}, u32[]{:S(2)}) copy-start(bf16[56,8192]{1,0:T(8,128)(2,1)} %param.11) | copy-start | bytes 2752516
  56.9 249.7 %all-gather.3.cloned.1.call-start = ((), (), s32[]{:S(2)}) async-start(), calls=%async_computation.6 | async-start | bytes 8650752 | tf_op jit(solution)/shard_map/all_gather | solution.py:39
  235.0 250.8 %reduce-scatter.5.cloned.1.call-start = ((), (), s32[]{:S(2)}) async-start(), calls=%async_computation.7 | async-start | bytes 278528 | tf_op jit(solution)/shard_map/reduce_scatter | solution.py:55
Sparse Core Ops, SparseCore 0:
  57.0 108.6 reduce-scatter.2
  235.1 71.4 all-gather.2
  378.6 107.1 reduce-scatter.4
